TPU v7x, 32 devices: a whole 2x2x4 slice. The times are simulated.
32 devices in a mesh: section: 2 (over x), expert: 16 (over z, y, core).
Axes of the slice: x: 2, y: 2, z: 4, core: 2. Of those that a mesh axis runs over, the one named last changes fastest.
Arguments:
- tokens: bfloat16 [2, 256, 2048], P('section', 'expert'), may hold values from -6 to 6
- out_grad: bfloat16 [2, 256, 2048], P('section', 'expert'), may hold values from -1 to 1
- expert_ids: int32 [2, 256, 2], P('section'), may hold values from 0 to 3, all different within a row; in each aligned block of 16 rows (0 to 15, 16 to 31, ..., all dimensions but the last counted through in order) at most 14 rows name the same one
- gate_weights: bfloat16 [2, 256, 2], P('section'), may hold values from 0.049804688 to 1
- gate_up_rows: bfloat16 [2, 16, 384, 2048], P('section', 'expert'), may hold values from -0.125 to 0.125
- down_rows: bfloat16 [2, 16, 192, 2048], P('section', 'expert'), may hold values from -0.21875 to 0.21875
Outputs:
- gate_grad: float32 [2, 256, 2], P('section', 'expert')
- handed: bfloat16 [2, 256, 2048], P('section', 'expert')
Inputs may be any that keep to these rules, and one draw needn't show every extreme that they name: `expert_ids`: within the rows of one device (16 consecutive rows of a section), every expert id appears in at most 14 rows, and some id reaches 14; the 2 ids of a row are distinct.
All inputs are finite; a program needn't handle non-finite values.
Results may differ from a plain program's by a relative error of at most 0.0049.
Values may be sent and summed in bfloat16 or wider, within the bound.
No kernel may reach another device: no remote copies, remote signals or barrier semaphores. Data moves between devices by JAX's collectives and lax.ppermute only.
A program may use at most 64 MiB of HBM per device.

v0:
```python
import jax
import jax.numpy as jnp
from jax import lax
from jax.sharding import PartitionSpec as P


def from_behind(shard, axis, by):
    length = lax.axis_size(axis)
    pairs = [(i, i + by) for i in range(length) if 0 <= i + by < length]
    return lax.ppermute(shard, axis, pairs)


def slot_table(matches, capacity):
    ranked = jnp.cumsum(matches, axis=-1) - 1.0
    levels = jnp.arange(capacity, dtype=jnp.float32)
    return matches[..., None, :] * (ranked[..., None, :] == levels[:, None]).astype(jnp.float32)


def expert_grads(rows_in, rows_grad, slot_gate, gate_up, down_mat):
    width = down_mat.shape[0]
    contract = (((1,), (1,)), ((), ()))
    both = lax.dot_general(rows_in, gate_up, contract, preferred_element_type=jnp.float32)
    first = both[:, :width]
    second = both[:, width:]
    back = lax.dot_general(rows_grad, down_mat, contract, preferred_element_type=jnp.float32)
    sigma = jax.nn.sigmoid(first)
    active = first * sigma
    slot_grad = jnp.sum(back * active * second, axis=1)
    scaled = slot_gate[:, None] * back
    d_first = scaled * second * sigma * (1.0 + first * (1.0 - sigma))
    d_second = scaled * active
    d_both = jnp.concatenate([d_first, d_second], axis=1).astype(jnp.bfloat16)
    contrib = jnp.dot(d_both, gate_up, preferred_element_type=jnp.float32)
    return (contrib, slot_grad)


def body(tokens, out_grad, expert_ids, gate_weights, gate_up_rows, down_rows):
    group_size = lax.axis_size("expert")
    expert_count = max(2, group_size // 4)
    part_count = group_size // expert_count
    position = lax.axis_index("expert")
    my_expert = position // part_count
    block_rows = tokens.shape[1]
    model_width = tokens.shape[2]
    route_count = expert_ids.shape[2]
    pairs = block_rows * route_count
    capacity = min(block_rows, max(2, 7 * block_rows * route_count // (4 * expert_count)))
    gate_up = gate_up_rows[0, 0]
    down_mat = down_rows[0, 0]
    all_ids = expert_ids[0]
    all_gates = gate_weights[0].astype(jnp.float32)
    highest = lax.Precision.HIGHEST
    all_in, all_grad = (
        lax.all_gather(tokens[0], "expert", axis=0, tiled=True),
        lax.all_gather(out_grad[0], "expert", axis=0, tiled=True),
    )
    matches = (all_ids.reshape(group_size, pairs) == my_expert).astype(jnp.float32)
    slot_pick = slot_table(matches, capacity)
    chooser = slot_pick.reshape(group_size, capacity, block_rows, route_count).sum(axis=-1)
    slot_gate = jnp.sum(slot_pick * all_gates.reshape(group_size, 1, pairs), axis=-1)
    chooser_half = chooser.astype(jnp.bfloat16)
    rows_in = jnp.einsum(
        "jrt,jtd->jrd",
        chooser_half,
        all_in.reshape(group_size, block_rows, model_width),
        preferred_element_type=jnp.float32,
    ).astype(jnp.bfloat16)
    rows_grad = jnp.einsum(
        "jrt,jtd->jrd",
        chooser_half,
        all_grad.reshape(group_size, block_rows, model_width),
        preferred_element_type=jnp.float32,
    ).astype(jnp.bfloat16)
    contrib, slot_grad = expert_grads(
        rows_in.reshape(-1, model_width),
        rows_grad.reshape(-1, model_width),
        slot_gate.reshape(-1),
        gate_up,
        down_mat,
    )
    partial_value = jnp.einsum(
        "jrt,jrd->jtd",
        chooser,
        contrib.reshape(group_size, capacity, model_width),
        precision=highest,
    ).reshape(group_size * block_rows, model_width)
    gate_part = jnp.einsum(
        "jrp,jr->jp", slot_pick, slot_grad.reshape(group_size, capacity), precision=highest
    ).reshape(group_size * block_rows, route_count)
    grad_rows, gate_grad = (
        lax.psum_scatter(partial_value, "expert", scatter_dimension=0, tiled=True),
        lax.psum_scatter(gate_part, "expert", scatter_dimension=0, tiled=True),
    )
    handed = from_behind(grad_rows.astype(jnp.bfloat16), "section", -1)
    return (gate_grad[None], handed[None])


def solution(mesh):
    return jax.shard_map(
        body,
        mesh=mesh,
        in_specs=(
            P("section", "expert", None),
            P("section", "expert", None),
            P("section", None, None),
            P("section", None, None),
            P("section", "expert", None, None),
            P("section", "expert", None, None),
        ),
        out_specs=(P("section", "expert", None), P("section", "expert", None)),
        check_vma=False,
    )
```

profile of v0, /device:TPU:0, one launch (start us, length us, event | category | flops | bytes accessed | tf_op | source)
XLA Modules:
  0.0 227.0 jit_solution(1445343976378787823)
XLA Ops:
  7.2 0.0 copy-start
  7.2 0.0 all-gather.7.cloned.1.call-start
  7.2 0.7 all-gather.7.cloned.1.call-update
  7.9 0.0 all-gather.5.cloned.1.call-start
  8.0 0.7 all-gather.5.cloned.1.call-update
  8.7 0.0 reduce-scatter.5.cloned.1.call-start
  8.7 0.7 compare_convert_fusion
  9.4 0.1 reshape.92
  9.5 0.1 copy.39
  9.6 0.1 reshape.91
  9.7 0.1 reshape.90
  9.9 0.2 reduce_window_sum.11
  10.1 0.1 copy.41
  10.1 0.1 copy.42
  10.3 0.6 copy-done.1
  10.9 0.0 copy-start.4
  10.9 0.8 copy.48
  11.8 0.1 reshape.93
  11.9 0.7 multiply_reduce_fusion.1
  12.5 0.1 copy.49
  12.6 0.1 mul.63
  12.7 38.2 %all-gather.7.cloned.1.call-done = bf16[1,256,2048]{2,1,0:T(8,128)(2,1)} async-done(((bf16[1,16,2048]{2,1,0:T(8,128)(2,1)}), bf16[1,256,2048]{2,1,0:T(8,128)(2,1)}) %all-gather.7.cloned.1.call-update) | async-done | bytes 1048592 | tf_op jit(solution)/shard_map/all_gather | solution.py:54
  50.9 1.6 convolution_convert_fusion
  52.5 0.3 reshape.86
  52.8 37.1 %all-gather.5.cloned.1.call-done = bf16[1,256,2048]{2,1,0:T(8,128)(2,1)} async-done(((bf16[1,16,2048]{2,1,0:T(8,128)(2,1)}), bf16[1,256,2048]{2,1,0:T(8,128)(2,1)}) %all-gather.5.cloned.1.call-update) | async-done | bytes 1048592 | tf_op jit(solution)/shard_map/all_gather | solution.py:55
  89.9 1.7 convolution_convert_fusion.1
  91.6 1.2 reshape.84
  92.8 0.6 fusion.2
  93.4 0.6 copy-done.3
  94.0 0.2 copy-done.6
  94.2 0.5 multiply_convert_fusion.1
  94.7 0.1 copy.50
  94.8 0.1 copy.51
  95.0 0.7 fusion
  95.8 0.1 copy-done.2
  95.8 3.3 %fusion.12 = f32[16,16,2048]{2,1,0:T(8,128)} fusion(f32[16,14,2048]{2,1,0:T(8,128)S(1)} %fusion, f32[16,14,16]{2,0,1:T(8,128)S(1)} %copy-done.2), kind=kOutput, calls=%fused_computation.20 | convolution fusion | flops 88080384 | bytes 3946496 | tf_op jit(solution)/shard_map/jrt,jrd->jtd/dot_general | solution.py:81
  99.1 0.0 reduce-scatter.5.cloned.1.call-update
  99.2 0.0 reduce-scatter.3.cloned.1.call-start
  99.2 0.1 reshape.98
  99.3 60.5 %reduce-scatter.5.cloned.1.call-done = f32[16,2048]{1,0:T(8,128)} async-done(((f32[256,2048]{1,0:T(8,128)}), f32[16,2048]{1,0:T(8,128)}) %reduce-scatter.5.cloned.1.call-update) | async-done | bytes 131088 | tf_op jit(solution)/shard_map/reduce_scatter | solution.py:91
  159.8 0.9 convert_element_type.62
  160.7 1.3 collective-permute-start
  162.0 0.3 fusion.10
  162.3 0.7 reshape.88
  163.1 0.0 reduce-scatter.3.cloned.1.call-update
  163.1 55.4 %reduce-scatter.3.cloned.1.call-done = f32[16,2]{1,0:T(8,128)} async-done(((f32[256,2]{1,0:T(8,128)}), f32[16,2]{1,0:T(8,128)}) %reduce-scatter.3.cloned.1.call-update) | async-done | bytes 144 | tf_op jit(solution)/shard_map/reduce_scatter | solution.py:92
  218.5 1.3 copy.47
  219.8 0.6 copy.66
  (14 shorter events, 0.2 us)
Async XLA Ops:
  7.2 85.6 %copy-start = (bf16[1,1,384,2048]{3,2,1,0:T(8,128)(2,1)S(1)}, bf16[1,1,384,2048]{3,2,1,0:T(8,128)(2,1)}, u32[]{:S(2)}) copy-start(bf16[1,1,384,2048]{3,2,1,0:T(8,128)(2,1)} %param.10) | copy-start | bytes 4718596
  7.2 43.7 %all-gather.7.cloned.1.call-start = ((), (), s32[]{:S(2)}) async-start(), calls=%async_computation.5 | async-start | bytes 1114112 | tf_op jit(solution)/shard_map/all_gather | solution.py:54
  7.9 82.0 %all-gather.5.cloned.1.call-start = ((), (), s32[]{:S(2)}) async-start(), calls=%async_computation.4 | async-start | bytes 1114112 | tf_op jit(solution)/shard_map/all_gather | solution.py:55
  8.7 151.2 %reduce-scatter.5.cloned.1.call-start = ((), (), s32[]{:S(2)}) async-start(), calls=%async_computation.3 | async-start | bytes 2228224 | tf_op jit(solution)/shard_map/reduce_scatter | solution.py:91
  10.3 0.7 copy-start.1
  10.9 39.9 %copy-start.4 = (bf16[16,14,16]{2,0,1:T(8,128)(2,1)}, bf16[16,14,16]{2,0,1:T(8,128)(2,1)S(1)}, u32[]{:S(2)}) copy-start(bf16[16,14,16]{2,0,1:T(8,128)(2,1)S(1)} %convert_element_type.57) | copy-start | bytes 21508
  92.8 1.2 copy-start.3
  92.8 1.4 copy-start.6
  94.9 0.9 copy-start.2
  99.1 62.9 %copy-start.5 = (f32[16,14,32]{2,0,1:T(8,128)S(1)}, f32[16,14,32]{2,0,1:T(8,128)}, u32[]{:S(2)}) copy-start(f32[16,14,32]{2,0,1:T(8,128)} %get-tuple-element.6) | copy-start | bytes 86020
  99.2 119.3 %reduce-scatter.3.cloned.1.call-start = ((), (), s32[]{:S(2)}) async-start(), calls=%async_computation.2 | async-start | bytes 139264 | tf_op jit(solution)/shard_map/reduce_scatter | solution.py:92
  160.7 59.1 %collective-permute-start = (bf16[16,2048]{1,0:T(8,128)(2,1)S(1)}, bf16[16,2048]{1,0:T(8,128)(2,1)S(1)}, u32[]{:S(2)}, u32[]{:S(2)}) collective-permute-start(bf16[16,2048]{1,0:T(8,128)(2,1)S(1)} %convert_element_type.62), channel_id=1, source_target_pairs={{16,0},{17,1},{18,2},{19,3},{20,4},{21,5},{22,6},{23,7},{24,8},{25... | collective-permute-start | bytes 196616 | tf_op jit(solution)/shard_map/ppermute | solution.py:10
Sparse Core Ops, SparseCore 0:
  10.2 40.6 all-gather.6
  53.0 36.8 all-gather.4
  99.3 60.4 reduce-scatter.4
  163.5 54.9 reduce-scatter.2
where the time goes:
time: 227 us
  waiting for transfers between devices  193 us (85%)
  between operations  13.9 us (6%)
  matrix products  8.71 us (4%)
  local copies, waits for them, and re-layouts  7.79 us (3%)
  other arithmetic  2.49 us (1%)
    reduce_scatter x1, waiting for transfers between devices, body(): lax.psum_scatter(partial_value, 'expert', scatter_dimension=0, tiled=True)  60.5 us
    reduce_scatter x1, waiting for transfers between devices, body(): lax.psum_scatter(gate_part, 'expert', scatter_dimension=0, tiled=True)  55.4 us
    all_gather x1, waiting for transfers between devices, body(): lax.all_gather(tokens[0], 'expert', axis=0, tiled=True)  38.2 us
    all_gather x1, waiting for transfers between devices, body(): lax.all_gather(out_grad[0], 'expert', axis=0, tiled=True)  37.1 us
  transfers between devices with their start and end apart: 5, of which 4 were waited for; matrix products, arithmetic and copies ran while one was open for 3% of the time, Pallas kernels for 0%

commit v1 on v0

--- a/solution.py
+++ b/solution.py
@@ -2,6 +2,22 @@
 import jax.numpy as jnp
 from jax import lax
 from jax.sharding import PartitionSpec as P
+
+
+def gather_around(x, axis, dim):
+    ways, here, step = (lax.axis_size(axis), lax.axis_index(axis), x.shape[dim])
+    lengths = [n * ways if d == dim else n for d, n in enumerate(x.shape)]
+    full = lax.dynamic_update_slice_in_dim(jnp.zeros(lengths, x.dtype), x, here * step, axis=dim)
+    going_up = going_down = x
+    for far in range(1, ways // 2 + 1):
+        going_up = lax.ppermute(going_up, axis, [(d, (d + 1) % ways) for d in range(ways)])
+        full = lax.dynamic_update_slice_in_dim(full, going_up, (here - far) % ways * step, axis=dim)
+        if 2 * far < ways:
+            going_down = lax.ppermute(going_down, axis, [(d, (d - 1) % ways) for d in range(ways)])
+            full = lax.dynamic_update_slice_in_dim(
+                full, going_down, (here + far) % ways * step, axis=dim
+            )
+    return full
 
 
 def from_behind(shard, axis, by):
@@ -51,7 +67,7 @@
     all_gates = gate_weights[0].astype(jnp.float32)
     highest = lax.Precision.HIGHEST
     all_in, all_grad = (
-        lax.all_gather(tokens[0], "expert", axis=0, tiled=True),
+        gather_around(tokens[0], "expert", 0),
         lax.all_gather(out_grad[0], "expert", axis=0, tiled=True),
     )
     matches = (all_ids.reshape(group_size, pairs) == my_expert).astype(jnp.float32)

time: 227 us -> 202 us (0.89)
  waiting for transfers between devices: 193 us -> 134 us
  starting transfers between devices: 1.44 us -> 34.5 us
    all_gather x1 -> x0, waiting for transfers between devices: 38.2 us -> none  [body(): lax.all_gather(tokens[0], 'expert', axis=0, tiled=True)]
    all_gather x1, waiting for transfers between devices: 37.1 us -> 0.02 us  [body(): lax.all_gather(out_grad[0], 'expert', axis=0, tiled=True)]
    ppermute x0 -> x15, starting transfers between devices: none -> 33.1 us  [the longest x7 32.5 us: gather_around(): lax.ppermute(going_down, axis, [(d, (d - 1) % ways) for d in range(ways)])]
    ppermute x0 -> x15, waiting for transfers between devices: none -> 17.7 us  [the longest x8 16 us: gather_around(): lax.ppermute(going_up, axis, [(d, (d + 1) % ways) for d in range(ways)])]
  transfers between devices with their start and end apart: 5 -> 19, of which waited for: 4 -> 15; matrix products, arithmetic and copies ran while one was open for 3% -> 4% of each run, Pallas kernels for 0% -> 0%
where the time goes in v1:
time: 202 us
  waiting for transfers between devices  134 us (66%)
  starting transfers between devices  34.5 us (17%)
  between operations  14.4 us (7%)
  matrix products  9.89 us (5%)
  local copies, waits for them, and re-layouts  7.67 us (4%)
    reduce_scatter x1, waiting for transfers between devices, body(): lax.psum_scatter(partial_value, 'expert', scatter_dimension=0, tiled=True)  60.6 us
    reduce_scatter x1, waiting for transfers between devices, body(): lax.psum_scatter(gate_part, 'expert', scatter_dimension=0, tiled=True)  55.4 us
    ppermute x7, starting transfers between devices, gather_around(): lax.ppermute(going_down, axis, [(d, (d - 1) % ways) for d in range(ways)])  32.5 us
    ppermute x8, waiting for transfers between devices, gather_around(): lax.ppermute(going_up, axis, [(d, (d + 1) % ways) for d in range(ways)])  16 us
  transfers between devices with their start and end apart: 19, of which 15 were waited for; matrix products, arithmetic and copies ran while one was open for 4% of the time, Pallas kernels for 0%

profile of v1, /device:TPU:0, one launch (start us, length us, event | category | flops | bytes accessed | tf_op | source)
XLA Modules:
  0.0 202.1 jit_solution(15090596092409772892)
XLA Ops:
  7.2 0.5 collective-permute-start
  7.7 5.1 %collective-permute-start.1 = (bf16[16,2048]{1,0:T(8,128)(2,1)}, bf16[16,2048]{1,0:T(8,128)(2,1)S(1)}, u32[]{:S(2)}, u32[]{:S(2)}) collective-permute-start(bf16[16,2048]{1,0:T(8,128)(2,1)} %bitcast.37), channel_id=1, source_target_pairs={{0,15},{1,0},{2,1},{3,2},{4,3},{5,4},{6,5},{7,6},{8,7},{9,8},{10,9... | collective-permute-start | bytes 196616 | tf_op jit(solution)/shard_map/ppermute | solution.py:16
  13.2 0.7 compare_convert_fusion
  13.9 0.1 copy.39
  14.1 0.1 reshape.91
  14.2 0.1 reshape.90
  14.3 0.2 reduce_window_sum.11
  14.6 0.8 copy.48
  15.5 0.1 reshape.93
  15.6 0.1 broadcast_in_dim.11
  15.7 0.1 multiply_reduce_fusion.1
  16.2 4.4 %collective-permute-start.3 = (bf16[16,2048]{1,0:T(8,128)(2,1)S(1)}, bf16[16,2048]{1,0:T(8,128)(2,1)S(1)}, u32[]{:S(2)}, u32[]{:S(2)}) collective-permute-start(bf16[16,2048]{1,0:T(8,128)(2,1)S(1)} %collective-permute-done.1), channel_id=1, source_target_pairs={{0,15},{1,0},{2,1},{3,2},{4,3},{5,4},{6,5},{7,6},{8,7},{9,8},{10,9... | collective-permute-start | bytes 196616 | tf_op jit(solution)/shard_map/ppermute | solution.py:16
  20.7 1.9 collective-permute-done.2
  22.6 0.2 collective-permute-done.3
  22.8 4.7 %collective-permute-start.5 = (bf16[16,2048]{1,0:T(8,128)(2,1)S(1)}, bf16[16,2048]{1,0:T(8,128)(2,1)S(1)}, u32[]{:S(2)}, u32[]{:S(2)}) collective-permute-start(bf16[16,2048]{1,0:T(8,128)(2,1)S(1)} %collective-permute-done.3), channel_id=1, source_target_pairs={{0,15},{1,0},{2,1},{3,2},{4,3},{5,4},{6,5},{7,6},{8,7},{9,8},{10,9... | collective-permute-start | bytes 196616 | tf_op jit(solution)/shard_map/ppermute | solution.py:16
  27.5 1.6 collective-permute-done.4
  29.1 0.2 collective-permute-done.5
  29.3 4.7 %collective-permute-start.7 = (bf16[16,2048]{1,0:T(8,128)(2,1)S(1)}, bf16[16,2048]{1,0:T(8,128)(2,1)S(1)}, u32[]{:S(2)}, u32[]{:S(2)}) collective-permute-start(bf16[16,2048]{1,0:T(8,128)(2,1)S(1)} %collective-permute-done.5), channel_id=1, source_target_pairs={{0,15},{1,0},{2,1},{3,2},{4,3},{5,4},{6,5},{7,6},{8,7},{9,8},{10,9... | collective-permute-start | bytes 196616 | tf_op jit(solution)/shard_map/ppermute | solution.py:16
  34.0 1.4 collective-permute-done.6
  35.5 0.4 collective-permute-done.7
  35.9 4.5 %collective-permute-start.9 = (bf16[16,2048]{1,0:T(8,128)(2,1)S(1)}, bf16[16,2048]{1,0:T(8,128)(2,1)S(1)}, u32[]{:S(2)}, u32[]{:S(2)}) collective-permute-start(bf16[16,2048]{1,0:T(8,128)(2,1)S(1)} %collective-permute-done.7), channel_id=1, source_target_pairs={{0,15},{1,0},{2,1},{3,2},{4,3},{5,4},{6,5},{7,6},{8,7},{9,8},{10,9... | collective-permute-start | bytes 196616 | tf_op jit(solution)/shard_map/ppermute | solution.py:16
  40.4 1.6 collective-permute-done.8
  42.0 0.5 collective-permute-done.9
  42.5 4.7 %collective-permute-start.11 = (bf16[16,2048]{1,0:T(8,128)(2,1)S(1)}, bf16[16,2048]{1,0:T(8,128)(2,1)S(1)}, u32[]{:S(2)}, u32[]{:S(2)}) collective-permute-start(bf16[16,2048]{1,0:T(8,128)(2,1)S(1)} %collective-permute-done.9), channel_id=1, source_target_pairs={{0,15},{1,0},{2,1},{3,2},{4,3},{5,4},{6,5},{7,6},{8,7},{9,8},{10,9... | collective-permute-start | bytes 196616 | tf_op jit(solution)/shard_map/ppermute | solution.py:16
  47.1 1.7 collective-permute-done.10
  48.8 0.2 collective-permute-done.11
  49.0 4.6 %collective-permute-start.13 = (bf16[16,2048]{1,0:T(8,128)(2,1)S(1)}, bf16[16,2048]{1,0:T(8,128)(2,1)S(1)}, u32[]{:S(2)}, u32[]{:S(2)}) collective-permute-start(bf16[16,2048]{1,0:T(8,128)(2,1)S(1)} %collective-permute-done.11), channel_id=1, source_target_pairs={{0,15},{1,0},{2,1},{3,2},{4,3},{5,4},{6,5},{7,6},{8,7},{9,8},{10,9... | collective-permute-start | bytes 196616 | tf_op jit(solution)/shard_map/ppermute | solution.py:16
  53.6 1.6 collective-permute-done.12
  55.2 0.3 collective-permute-done.13
  55.5 6.1 %collective-permute-done.14 = bf16[16,2048]{1,0:T(8,128)(2,1)S(1)} collective-permute-done((bf16[16,2048]{1,0:T(8,128)(2,1)S(1)}, bf16[16,2048]{1,0:T(8,128)(2,1)S(1)}, u32[]{:S(2)}, u32[]{:S(2)}) %collective-permute-start.14) | collective-permute-done | bytes 65568 | tf_op jit(solution)/shard_map/ppermute | solution.py:13
  61.6 1.4 convolution_convert_fusion
  63.0 1.4 reshape.86
  64.5 0.6 fusion.2
  65.1 1.6 convolution_convert_fusion.1
  66.8 1.2 reshape.84
  68.0 1.9 multiply_convert_fusion.1
  69.9 0.1 copy.50
  70.0 0.1 copy.51
  70.2 0.7 fusion
  70.9 3.3 %fusion.12 = f32[16,16,2048]{2,1,0:T(8,128)} fusion(f32[16,14,2048]{2,1,0:T(8,128)S(1)} %fusion, f32[16,14,16]{2,0,1:T(8,128)S(1)} %select_reduce_fusion), kind=kOutput, calls=%fused_computation.20 | convolution fusion | flops 88080384 | bytes 3946496 | tf_op jit(solution)/shard_map/jrt,jrd->jtd/dot_general | solution.py:97
  74.4 60.6 %reduce-scatter.5.cloned.1.call-done = f32[16,2048]{1,0:T(8,128)} async-done(((f32[256,2048]{1,0:T(8,128)}), f32[16,2048]{1,0:T(8,128)}) %reduce-scatter.5.cloned.1.call-update) | async-done | bytes 131088 | tf_op jit(solution)/shard_map/reduce_scatter | solution.py:107
  135.0 0.9 convert_element_type.62
  135.9 1.3 collective-permute-start.15
  137.2 0.3 fusion.10
  137.5 0.8 reshape.88
  138.2 55.4 %reduce-scatter.3.cloned.1.call-done = f32[16,2]{1,0:T(8,128)} async-done(((f32[256,2]{1,0:T(8,128)}), f32[16,2]{1,0:T(8,128)}) %reduce-scatter.3.cloned.1.call-update) | async-done | bytes 144 | tf_op jit(solution)/shard_map/reduce_scatter | solution.py:108
  193.6 1.3 copy.47
  195.0 0.6 copy.82
  (48 shorter events, 1.1 us)
Async XLA Ops:
  7.2 57.3 %copy-start = (bf16[1,1,384,2048]{3,2,1,0:T(8,128)(2,1)S(1)}, bf16[1,1,384,2048]{3,2,1,0:T(8,128)(2,1)}, u32[]{:S(2)}) copy-start(bf16[1,1,384,2048]{3,2,1,0:T(8,128)(2,1)} %param.10) | copy-start | bytes 4718596
  7.2 8.5 %copy-start.1 = (bf16[1,16,2048]{2,1,0:T(8,128)(2,1)S(1)}, bf16[1,16,2048]{2,1,0:T(8,128)(2,1)}, u32[]{:S(2)}) copy-start(bf16[1,16,2048]{2,1,0:T(8,128)(2,1)} %param.6) | copy-start | bytes 196612
  7.2 57.9 %all-gather.3.cloned.1.call-start = ((), (), s32[]{:S(2)}) async-start(), calls=%async_computation.4 | async-start | bytes 1114112 | tf_op jit(solution)/shard_map/all_gather | solution.py:71
  7.2 8.9 %collective-permute-start = (bf16[16,2048]{1,0:T(8,128)(2,1)}, bf16[16,2048]{1,0:T(8,128)(2,1)S(1)}, u32[]{:S(2)}, u32[]{:S(2)}) collective-permute-start(bf16[16,2048]{1,0:T(8,128)(2,1)} %bitcast.36), channel_id=1, source_target_pairs={{0,1},{1,2},{2,3},{3,4},{4,5},{5,6},{6,7},{7,8},{8,9},{9,10},{10,1... | collective-permute-start | bytes 196616 | tf_op jit(solution)/shard_map/ppermute | solution.py:13
  7.7 8.5 %collective-permute-start.1 = (bf16[16,2048]{1,0:T(8,128)(2,1)}, bf16[16,2048]{1,0:T(8,128)(2,1)S(1)}, u32[]{:S(2)}, u32[]{:S(2)}) collective-permute-start(bf16[16,2048]{1,0:T(8,128)(2,1)} %bitcast.37), channel_id=1, source_target_pairs={{0,15},{1,0},{2,1},{3,2},{4,3},{5,4},{6,5},{7,6},{8,7},{9,8},{10,9... | collective-permute-start | bytes 196616 | tf_op jit(solution)/shard_map/ppermute | solution.py:16
  12.8 122.1 %reduce-scatter.5.cloned.1.call-start = ((), (), s32[]{:S(2)}) async-start(), calls=%async_computation.3 | async-start | bytes 2228224 | tf_op jit(solution)/shard_map/reduce_scatter | solution.py:107
  16.1 6.5 %collective-permute-start.2 = (bf16[16,2048]{1,0:T(8,128)(2,1)S(1)}, bf16[16,2048]{1,0:T(8,128)(2,1)S(1)}, u32[]{:S(2)}, u32[]{:S(2)}) collective-permute-start(bf16[16,2048]{1,0:T(8,128)(2,1)S(1)} %collective-permute-done), channel_id=1, source_target_pairs={{0,1},{1,2},{2,3},{3,4},{4,5},{5,6},{6,7},{7,8},{8,9},{9,10},{10,1... | collective-permute-start | bytes 196616 | tf_op jit(solution)/shard_map/ppermute | solution.py:13
  16.2 6.5 %collective-permute-start.3 = (bf16[16,2048]{1,0:T(8,128)(2,1)S(1)}, bf16[16,2048]{1,0:T(8,128)(2,1)S(1)}, u32[]{:S(2)}, u32[]{:S(2)}) collective-permute-start(bf16[16,2048]{1,0:T(8,128)(2,1)S(1)} %collective-permute-done.1), channel_id=1, source_target_pairs={{0,15},{1,0},{2,1},{3,2},{4,3},{5,4},{6,5},{7,6},{8,7},{9,8},{10,9... | collective-permute-start | bytes 196616 | tf_op jit(solution)/shard_map/ppermute | solution.py:16
  22.6 6.5 %collective-permute-start.4 = (bf16[16,2048]{1,0:T(8,128)(2,1)S(1)}, bf16[16,2048]{1,0:T(8,128)(2,1)S(1)}, u32[]{:S(2)}, u32[]{:S(2)}) collective-permute-start(bf16[16,2048]{1,0:T(8,128)(2,1)S(1)} %collective-permute-done.2), channel_id=1, source_target_pairs={{0,1},{1,2},{2,3},{3,4},{4,5},{5,6},{6,7},{7,8},{8,9},{9,10},{10,1... | collective-permute-start | bytes 196616 | tf_op jit(solution)/shard_map/ppermute | solution.py:13
  22.8 6.6 %collective-permute-start.5 = (bf16[16,2048]{1,0:T(8,128)(2,1)S(1)}, bf16[16,2048]{1,0:T(8,128)(2,1)S(1)}, u32[]{:S(2)}, u32[]{:S(2)}) collective-permute-start(bf16[16,2048]{1,0:T(8,128)(2,1)S(1)} %collective-permute-done.3), channel_id=1, source_target_pairs={{0,15},{1,0},{2,1},{3,2},{4,3},{5,4},{6,5},{7,6},{8,7},{9,8},{10,9... | collective-permute-start | bytes 196616 | tf_op jit(solution)/shard_map/ppermute | solution.py:16
  29.1 6.4 %collective-permute-start.6 = (bf16[16,2048]{1,0:T(8,128)(2,1)S(1)}, bf16[16,2048]{1,0:T(8,128)(2,1)S(1)}, u32[]{:S(2)}, u32[]{:S(2)}) collective-permute-start(bf16[16,2048]{1,0:T(8,128)(2,1)S(1)} %collective-permute-done.4), channel_id=1, source_target_pairs={{0,1},{1,2},{2,3},{3,4},{4,5},{5,6},{6,7},{7,8},{8,9},{9,10},{10,1... | collective-permute-start | bytes 196616 | tf_op jit(solution)/shard_map/ppermute | solution.py:13
  29.3 6.6 %collective-permute-start.7 = (bf16[16,2048]{1,0:T(8,128)(2,1)S(1)}, bf16[16,2048]{1,0:T(8,128)(2,1)S(1)}, u32[]{:S(2)}, u32[]{:S(2)}) collective-permute-start(bf16[16,2048]{1,0:T(8,128)(2,1)S(1)} %collective-permute-done.5), channel_id=1, source_target_pairs={{0,15},{1,0},{2,1},{3,2},{4,3},{5,4},{6,5},{7,6},{8,7},{9,8},{10,9... | collective-permute-start | bytes 196616 | tf_op jit(solution)/shard_map/ppermute | solution.py:16
  35.5 6.5 %collective-permute-start.8 = (bf16[16,2048]{1,0:T(8,128)(2,1)S(1)}, bf16[16,2048]{1,0:T(8,128)(2,1)S(1)}, u32[]{:S(2)}, u32[]{:S(2)}) collective-permute-start(bf16[16,2048]{1,0:T(8,128)(2,1)S(1)} %collective-permute-done.6), channel_id=1, source_target_pairs={{0,1},{1,2},{2,3},{3,4},{4,5},{5,6},{6,7},{7,8},{8,9},{9,10},{10,1... | collective-permute-start | bytes 196616 | tf_op jit(solution)/shard_map/ppermute | solution.py:13
  35.9 6.6 %collective-permute-start.9 = (bf16[16,2048]{1,0:T(8,128)(2,1)S(1)}, bf16[16,2048]{1,0:T(8,128)(2,1)S(1)}, u32[]{:S(2)}, u32[]{:S(2)}) collective-permute-start(bf16[16,2048]{1,0:T(8,128)(2,1)S(1)} %collective-permute-done.7), channel_id=1, source_target_pairs={{0,15},{1,0},{2,1},{3,2},{4,3},{5,4},{6,5},{7,6},{8,7},{9,8},{10,9... | collective-permute-start | bytes 196616 | tf_op jit(solution)/shard_map/ppermute | solution.py:16
  42.0 6.8 %collective-permute-start.10 = (bf16[16,2048]{1,0:T(8,128)(2,1)S(1)}, bf16[16,2048]{1,0:T(8,128)(2,1)S(1)}, u32[]{:S(2)}, u32[]{:S(2)}) collective-permute-start(bf16[16,2048]{1,0:T(8,128)(2,1)S(1)} %collective-permute-done.8), channel_id=1, source_target_pairs={{0,1},{1,2},{2,3},{3,4},{4,5},{5,6},{6,7},{7,8},{8,9},{9,10},{10,1... | collective-permute-start | bytes 196616 | tf_op jit(solution)/shard_map/ppermute | solution.py:13
  42.5 6.6 %collective-permute-start.11 = (bf16[16,2048]{1,0:T(8,128)(2,1)S(1)}, bf16[16,2048]{1,0:T(8,128)(2,1)S(1)}, u32[]{:S(2)}, u32[]{:S(2)}) collective-permute-start(bf16[16,2048]{1,0:T(8,128)(2,1)S(1)} %collective-permute-done.9), channel_id=1, source_target_pairs={{0,15},{1,0},{2,1},{3,2},{4,3},{5,4},{6,5},{7,6},{8,7},{9,8},{10,9... | collective-permute-start | bytes 196616 | tf_op jit(solution)/shard_map/ppermute | solution.py:16
  48.8 6.4 %collective-permute-start.12 = (bf16[16,2048]{1,0:T(8,128)(2,1)S(1)}, bf16[16,2048]{1,0:T(8,128)(2,1)S(1)}, u32[]{:S(2)}, u32[]{:S(2)}) collective-permute-start(bf16[16,2048]{1,0:T(8,128)(2,1)S(1)} %collective-permute-done.10), channel_id=1, source_target_pairs={{0,1},{1,2},{2,3},{3,4},{4,5},{5,6},{6,7},{7,8},{8,9},{9,10},{10,1... | collective-permute-start | bytes 196616 | tf_op jit(solution)/shard_map/ppermute | solution.py:13
  49.0 6.5 %collective-permute-start.13 = (bf16[16,2048]{1,0:T(8,128)(2,1)S(1)}, bf16[16,2048]{1,0:T(8,128)(2,1)S(1)}, u32[]{:S(2)}, u32[]{:S(2)}) collective-permute-start(bf16[16,2048]{1,0:T(8,128)(2,1)S(1)} %collective-permute-done.11), channel_id=1, source_target_pairs={{0,15},{1,0},{2,1},{3,2},{4,3},{5,4},{6,5},{7,6},{8,7},{9,8},{10,9... | collective-permute-start | bytes 196616 | tf_op jit(solution)/shard_map/ppermute | solution.py:16
  55.2 6.4 %collective-permute-start.14 = (bf16[16,2048]{1,0:T(8,128)(2,1)S(1)}, bf16[16,2048]{1,0:T(8,128)(2,1)S(1)}, u32[]{:S(2)}, u32[]{:S(2)}) collective-permute-start(bf16[16,2048]{1,0:T(8,128)(2,1)S(1)} %collective-permute-done.12), channel_id=1, source_target_pairs={{0,1},{1,2},{2,3},{3,4},{4,5},{5,6},{6,7},{7,8},{8,9},{9,10},{10,1... | collective-permute-start | bytes 196616 | tf_op jit(solution)/shard_map/ppermute | solution.py:13
  74.3 119.4 %reduce-scatter.3.cloned.1.call-start = ((), (), s32[]{:S(2)}) async-start(), calls=%async_computation.2 | async-start | bytes 139264 | tf_op jit(solution)/shard_map/reduce_scatter | solution.py:108
  135.9 59.1 %collective-permute-start.15 = (bf16[16,2048]{1,0:T(8,128)(2,1)S(1)}, bf16[16,2048]{1,0:T(8,128)(2,1)S(1)}, u32[]{:S(2)}, u32[]{:S(2)}) collective-permute-start(bf16[16,2048]{1,0:T(8,128)(2,1)S(1)} %convert_element_type.62), channel_id=1, source_target_pairs={{16,0},{17,1},{18,2},{19,3},{20,4},{21,5},{22,6},{23,7},{24,8},{25... | collective-permute-start | bytes 196616 | tf_op jit(solution)/shard_map/ppermute | solution.py:26
Sparse Core Ops, SparseCore 0:
  12.9 39.1 all-gather.2
  74.4 60.5 reduce-scatter.4
  138.8 54.7 reduce-scatter.2
